TPU v7x, 32 devices: a whole 2x2x4 slice. The times are simulated.
32 devices in a mesh: dp: 1, fsdp: 32 (over z, y, x, core).
Axes of the slice: x: 2, y: 2, z: 4, core: 2. Of those that a mesh axis runs over, the one named last changes fastest.
Arguments:
- hidden_states: bfloat16 [128, 4096], P(('dp', 'fsdp')), may hold values from -400 to 400
- token_ids: int32 [128], P(('dp', 'fsdp')), may hold values from 0 to 4095
- norm_gain: float32 [4096], replicated, may hold values from 0.5 to 1.5
- ref_gate_w: bfloat16 [4096, 14784], P('dp', 'fsdp'), may hold values from -0.1875 to 0.1875
- ref_up_w: bfloat16 [4096, 14784], P('dp', 'fsdp'), may hold values from -0.1875 to 0.1875
- ref_down_w: bfloat16 [14784, 4096], P('fsdp', 'dp'), may hold values from -0.09375 to 0.09375
- pol_gate_w: bfloat16 [4096, 14784], P('dp', 'fsdp'), may hold values from -0.1875 to 0.1875
- pol_up_w: bfloat16 [4096, 14784], P('dp', 'fsdp'), may hold values from -0.1875 to 0.1875
- pol_down_w: bfloat16 [14784, 4096], P('fsdp', 'dp'), may hold values from -0.09375 to 0.09375
- sample_lengths: int32 [1, 32], P('dp'), may hold values from 1 to 24, 128 in all within a row
- prompt_index: int32 [1, 32], P('dp'), may hold values from 0 to 3, as said below
- rewards: float32 [1, 32], P('dp'), may hold values from -6 to 6
Outputs:
- grad_gate: float32 [4096, 14784], P('dp', 'fsdp')
- grad_up: float32 [4096, 14784], P('dp', 'fsdp')
- grad_down: float32 [14784, 4096], P('fsdp', 'dp')
- advantage: float32 [1, 32], P('dp')
Inputs may be any that keep to these rules, and one draw needn't show every extreme that they name: `prompt_index`: in each row, every prompt from 0 to 3 is answered by exactly 8 samples. `sample_lengths`: each row sums to 128.
All inputs are finite; a program needn't handle non-finite values.
Results may differ from a plain program's by a relative error of at most 0.013.
Values may be sent and summed in bfloat16 or wider, within the bound.
No kernel may reach another device: no remote copies, remote signals or barrier semaphores. Data moves between devices by JAX's collectives and lax.ppermute only.
A program may use at most 128 MiB of HBM per device.

v0:
```python
import jax
import jax.numpy as jnp
from jax import lax
from jax.sharding import PartitionSpec as P

K = 8
EPSILON = 1e-06
KL_WEIGHT = 0.05


def combined_all(part, axis, combine):
    gathered = jax.tree.map(lambda a: lax.all_gather(a, axis), part)

    def take(source):
        return jax.tree.map(lambda a: lax.dynamic_index_in_dim(a, source, 0, False), gathered)

    return lax.fori_loop(
        1, lax.axis_size(axis), lambda source, state: combine(state, take(source)), take(0)
    )


def normalize(states, norm_gain):
    values = states.astype(jnp.float32)
    factor = lax.rsqrt(jnp.mean(values * values, axis=-1, keepdims=True) + EPSILON)
    return (values * factor * norm_gain).astype(jnp.bfloat16)


def combine_totals(first, second):
    row_peak = jnp.maximum(first[0], second[0])
    summed = first[1] * jnp.exp(first[0] - row_peak) + second[1] * jnp.exp(second[0] - row_peak)
    return (row_peak, summed, first[2] + second[2])


def column_section(normed_cols, state_cols, ids_all, weight_sets, group_index):
    col_width = state_cols.shape[1]
    unit_count = weight_sets[0][0].shape[1]
    in_weights = jnp.concatenate(
        [matrix for triple in weight_sets for matrix in triple[:2]], axis=1
    )
    row_block = normed_cols
    pre_sums = lax.psum_scatter(
        jnp.dot(row_block, in_weights, preferred_element_type=jnp.float32),
        "dp",
        scatter_dimension=0,
        tiled=True,
    )
    gate_pre = pre_sums[:, 0:unit_count]
    up_pre = pre_sums[:, unit_count : 2 * unit_count]
    activations = jax.nn.silu(gate_pre) * up_pre
    hidden_local = activations.astype(jnp.bfloat16)
    hidden_all = lax.all_gather(hidden_local, "dp", axis=0, tiled=True)
    row_block = hidden_all
    pieces = jnp.dot(row_block, weight_sets[0][2], preferred_element_type=jnp.float32)
    out_cols = lax.psum_scatter(pieces, "fsdp", scatter_dimension=0, tiled=True)
    states = state_cols.astype(jnp.float32)
    col_ids = jnp.arange(col_width, dtype=jnp.int32) + group_index * col_width
    logits = states + out_cols
    row_peak = jnp.max(logits, axis=1)
    logits_list = [logits]
    peaks = [row_peak]
    sums = [jnp.sum(jnp.exp(logits - row_peak[:, None]), axis=1)]
    picks = [jnp.sum(jnp.where(col_ids[None, :] == ids_all[:, None], logits, 0.0), axis=1)]
    row_peak, summed, picked = combined_all(
        (jnp.stack(peaks, axis=1), jnp.stack(sums, axis=1), jnp.stack(picks, axis=1)),
        "dp",
        combine_totals,
    )
    log_total = row_peak + jnp.log(summed)
    return (pre_sums, hidden_all, logits_list, log_total, picked - log_total)


def leave_one_out(log_gap, inside, prompt_index, rewards):
    divergence = lax.psum(jnp.sum(log_gap[:, None] * inside, axis=0), "fsdp")
    scores = rewards[0] - KL_WEIGHT * divergence
    same_prompt = (prompt_index[0][:, None] == prompt_index[0][None, :]).astype(jnp.float32)
    others = jnp.sum(same_prompt * scores[None, :], axis=1) - scores
    advantage = scores - others / (K - 1)
    weight = jnp.sum(inside * advantage[None, :], axis=1)
    return (advantage, weight)


def local(
    hidden_states,
    token_ids,
    norm_gain,
    ref_gate_w,
    ref_up_w,
    ref_down_w,
    pol_gate_w,
    pol_up_w,
    pol_down_w,
    sample_lengths,
    prompt_index,
    rewards,
):
    token_count = hidden_states.shape[0]
    model_width = hidden_states.shape[1]
    group_index = lax.axis_index("dp")
    member_index = lax.axis_index("fsdp")
    unit_count = pol_gate_w.shape[1]
    normed = normalize(hidden_states, norm_gain)
    normed_mixed, state_cols = (
        lax.all_to_all(normed, "dp", split_axis=1, concat_axis=0, tiled=True),
        lax.all_to_all(hidden_states, "dp", split_axis=1, concat_axis=0, tiled=True),
    )
    normed_cols = lax.all_gather(normed_mixed, "fsdp", axis=0, tiled=True)
    ids_all = lax.all_gather(token_ids, "dp", axis=0, tiled=True)
    own_start = group_index * token_count
    position = member_index * token_count + jnp.arange(token_count, dtype=jnp.int32)
    sample_ends = jnp.cumsum(sample_lengths[0])
    sample_starts = sample_ends - sample_lengths[0]
    inside = (
        (position[:, None] >= sample_starts[None, :]) & (position[:, None] < sample_ends[None, :])
    ).astype(jnp.float32)
    _, _, _, _, ref_lp = column_section(
        normed_cols, state_cols, ids_all, [(ref_gate_w, ref_up_w, ref_down_w)], group_index
    )
    ref_own = lax.dynamic_slice_in_dim(ref_lp[:, 0], own_start, token_count, 0)
    group_normed = lax.all_gather(normed, "fsdp", axis=0, tiled=True)
    row_block = group_normed
    gate_pre = jnp.dot(
        row_block,
        lax.all_gather(pol_gate_w, "dp", axis=0, tiled=True),
        preferred_element_type=jnp.float32,
    )
    up_pre = jnp.dot(
        row_block,
        lax.all_gather(pol_up_w, "dp", axis=0, tiled=True),
        preferred_element_type=jnp.float32,
    )
    down_full = lax.all_gather(pol_down_w, "dp", axis=1, tiled=True)
    hidden = (jax.nn.silu(gate_pre) * up_pre).astype(jnp.bfloat16)
    row_block = hidden
    pol_out = lax.psum_scatter(
        jnp.dot(row_block, down_full, preferred_element_type=jnp.float32),
        "fsdp",
        scatter_dimension=0,
        tiled=True,
    )
    logits = hidden_states.astype(jnp.float32) + pol_out
    row_peak = jnp.max(logits, axis=1)
    log_total = row_peak + jnp.log(jnp.sum(jnp.exp(logits - row_peak[:, None]), axis=1))
    columns = jnp.arange(model_width, dtype=jnp.int32)
    onehot = (columns[None, :] == token_ids[:, None]).astype(jnp.float32)
    pol_own = (
        jnp.sum(jnp.where(columns[None, :] == token_ids[:, None], logits, 0.0), axis=1) - log_total
    )
    advantage, weight = leave_one_out(pol_own - ref_own, inside, prompt_index, rewards)
    grad_logits = (-weight[:, None] * (onehot - jnp.exp(logits - log_total[:, None]))).astype(
        jnp.bfloat16
    )
    group_grads = lax.all_gather(grad_logits, "fsdp", axis=0, tiled=True)
    down_term = lax.dot_general(
        hidden, group_grads, (((0,), (0,)), ((), ())), preferred_element_type=jnp.float32
    )
    grad_down = lax.psum_scatter(
        down_term.astype(jnp.bfloat16), "dp", scatter_dimension=1, tiled=True
    ).astype(jnp.float32)
    grad_hidden = lax.dot_general(
        group_grads, down_full, (((1,), (1,)), ((), ())), preferred_element_type=jnp.float32
    )
    sigmoid_gate = jax.nn.sigmoid(gate_pre)
    grad_gate_pre = grad_hidden * up_pre * sigmoid_gate * (1.0 + gate_pre * (1.0 - sigmoid_gate))
    grad_up_pre = grad_hidden * gate_pre * sigmoid_gate
    gate_grads = jnp.concatenate(
        [grad_gate_pre.astype(jnp.bfloat16), grad_up_pre.astype(jnp.bfloat16)], axis=1
    )
    row_block = group_normed
    grad_inner = lax.psum_scatter(
        lax.dot_general(
            row_block, gate_grads, (((0,), (0,)), ((), ())), preferred_element_type=jnp.float32
        ).astype(jnp.bfloat16),
        "dp",
        scatter_dimension=0,
        tiled=True,
    ).astype(jnp.float32)
    return (grad_inner[:, :unit_count], grad_inner[:, unit_count:], grad_down, advantage[None, :])


def solution(mesh):
    return jax.shard_map(
        local,
        mesh=mesh,
        in_specs=(
            P(("dp", "fsdp"), None),
            P(("dp", "fsdp")),
            P(),
            P("dp", "fsdp"),
            P("dp", "fsdp"),
            P("fsdp", "dp"),
            P("dp", "fsdp"),
            P("dp", "fsdp"),
            P("fsdp", "dp"),
            P("dp", None),
            P("dp", None),
            P("dp", None),
        ),
        out_specs=(P("dp", "fsdp"), P("dp", "fsdp"), P("fsdp", "dp"), P("dp", None)),
        check_vma=False,
    )
```

profile of v0, /device:TPU:0, one launch (start us, length us, event | category | flops | bytes accessed | tf_op | source)
XLA Modules:
  0.0 356.7 jit_solution(6231580681784564363)
XLA Ops:
  7.2 0.9 fusion.12
  8.1 1.5 fusion.15
  9.7 58.1 %all-gather.5.cloned.1.call-done = bf16[32,4,4096]{2,1,0:T(4,128)(2,1)} async-done(((bf16[1,4,4096]{2,1,0:T(4,128)(2,1)}), bf16[32,4,4096]{2,1,0:T(4,128)(2,1)}) %all-gather.5.cloned.1.call-update) | async-done | bytes 1048592 | tf_op jit(solution)/shard_map/all_gather | solution.py:119
  67.8 1.3 reshape.84
  69.1 3.4 fusion.24
  72.5 1.2 multiply_convert_fusion.2
  73.7 0.9 copy-done
  74.6 2.1 fusion.25
  76.7 1.1 copy-done.8
  77.8 2.1 fusion
  80.0 2.1 fusion.9
  82.5 141.3 %all-reduce.5.cloned.1.call-done = (f32[128,4096]{1,0:T(8,128)}, f32[128,4096]{1,0:T(8,128)}) async-done(((f32[128,4096]{1,0:T(8,128)}, f32[128,4096]{1,0:T(8,128)}), (f32[128,4096]{1,0:T(8,128)}, f32[128,4096]{1,0:T(8,128)})) %all-reduce.5.cloned.1.call-update) | async-done | bytes 4194320
  223.8 1.1 fusion.17
  224.8 1.2 exponential_reduce_fusion
  226.1 1.1 exponential_reduce_fusion.1
  227.3 39.5 %psum.7 = f32[32]{0:T(128)S(1)} all-reduce(f32[32]{0:T(128)S(1)} %get-tuple-element.12), channel_id=1, replica_groups=mesh['dp'=1,'fsdp'=32] {'fsdp'}, use_global_device_ids=true, to_apply=%region_11.12 | all-reduce | flops 32 | bytes 256 | tf_op jit(solution)/shard_map/psum | solution.py:73
  266.9 0.2 select_reduce_fusion.2
  267.2 1.6 fusion.16
  268.8 53.2 %all-gather.7.cloned.1.call-done = bf16[32,4,4096]{2,1,0:T(4,128)(2,1)} async-done(((bf16[1,4,4096]{2,1,0:T(4,128)(2,1)}), bf16[32,4,4096]{2,1,0:T(4,128)(2,1)}) %all-gather.7.cloned.1.call-update) | async-done | bytes 1048592 | tf_op jit(solution)/shard_map/all_gather | solution.py:152
  322.1 1.3 reshape.86
  323.4 4.3 %fusion.4 = f32[462,4096]{1,0:T(8,128)} fusion(bf16[128,462]{0,1:T(8,128)(2,1)S(1)} %get-tuple-element.20, bf16[128,4096]{1,0:T(8,128)(2,1)S(1)} %reshape.86), kind=kOutput, calls=%fused_computation.6 | convolution fusion | flops 488226816 | bytes 8736256 | tf_op jit(solution)/shard_map/dot_general | solution.py:153
  327.7 1.1 multiply_convert_fusion.1
  328.8 7.5 %convert_convert_fusion = f32[4096,924]{0,1:T(8,128)} fusion(bf16[128,4096]{1,0:T(8,128)(2,1)S(1)} %reshape.84, bf16[128,462]{0,1:T(8,128)(2,1)S(1)} %get-tuple-element.19, bf16[128,462]{0,1:T(8,128)(2,1)S(1)} %get-tuple-element.18), kind=kOutput, calls=%fused_computation.4 | convolution fusion | flops 976926720 | bytes 16423936 | tf_op jit(solution)/shard_map/dot_general | solution.py:170
  336.3 13.9 %fusion.23 = (f32[4096,462]{0,1:T(8,128)}, f32[4096,462]{0,1:T(8,128)}) fusion(f32[4096,924]{0,1:T(8,128)} %convert_convert_fusion), kind=kLoop, calls=%fused_computation.50 | loop fusion | bytes 30277632 | tf_op jit(solution)/shard_map/slice | solution.py:177
  (40 shorter events, 0.7 us)
Async XLA Ops:
  7.2 60.6 %all-gather.5.cloned.1.call-start = ((), (), s32[]{:S(2)}) async-start(), calls=%async_computation | async-start | bytes 1081344 | tf_op jit(solution)/shard_map/all_gather | solution.py:119
  9.6 214.1 %all-reduce.5.cloned.1.call-start = ((), (), s32[]{:S(2)}) async-start(), calls=%async_computation.2 | async-start | bytes 8388608
  69.1 3.4 copy-start.2
  72.5 2.1 copy-start
  72.5 4.1 %copy-start.9 = (bf16[4096,462]{0,1:T(8,128)(2,1)S(1)}, bf16[4096,462]{0,1:T(8,128)(2,1)}, u32[]{:S(2)}) copy-start(bf16[4096,462]{0,1:T(8,128)(2,1)} %param.15) | copy-start | bytes 11354116
  73.7 4.1 %copy-start.8 = (bf16[4096,462]{0,1:T(8,128)(2,1)S(1)}, bf16[4096,462]{0,1:T(8,128)(2,1)}, u32[]{:S(2)}) copy-start(bf16[4096,462]{0,1:T(8,128)(2,1)} %param.16) | copy-start | bytes 11354116
  77.8 2.1 copy-start.3
  79.9 2.2 copy-start.7
  80.0 143.8 %copy-start.4 = (bf16[4,4096]{1,0:T(4,128)(2,1)S(1)}, bf16[4,4096]{1,0:T(4,128)(2,1)}, u32[]{:S(2)}) copy-start(bf16[4,4096]{1,0:T(4,128)(2,1)} %param.12) | copy-start | bytes 98308
  80.0 144.8 %copy-start.5 = (s32[4]{0:T(128)S(1)}, s32[4]{0:T(128)}, u32[]{:S(2)}) copy-start(s32[4]{0:T(128)} %param.13) | copy-start | bytes 52
  82.1 184.8 %copy-start.10 = (f32[1,32]{1,0:T(1,128)S(1)}, f32[1,32]{1,0:T(1,128)}, u32[]{:S(2)}) copy-start(f32[1,32]{1,0:T(1,128)} %param.23) | copy-start | bytes 388
  82.1 184.8 %copy-start.6 = (s32[1,32]{1,0:T(1,128)S(1)}, s32[1,32]{1,0:T(1,128)}, u32[]{:S(2)}) copy-start(s32[1,32]{1,0:T(1,128)} %param.22) | copy-start | bytes 388
  82.1 239.9 %all-gather.7.cloned.1.call-start = ((), (), s32[]{:S(2)}) async-start(), calls=%async_computation.1 | async-start | bytes 1081344 | tf_op jit(solution)/shard_map/all_gather | solution.py:152
  267.0 60.6 %copy-start.11 = (f32[32]{0:T(128)}, f32[32]{0:T(128)S(1)}, u32[]{:S(2)}) copy-start(f32[32]{0:T(128)S(1)} %multiply_subtract_fusion) | copy-start | bytes 388
  323.4 4.3 %copy-start.1 = (bf16[462,4096]{1,0:T(8,128)(2,1)S(1)}, bf16[462,4096]{1,0:T(8,128)(2,1)}, u32[]{:S(2)}) copy-start(bf16[462,4096]{1,0:T(8,128)(2,1)} %param.20) | copy-start | bytes 11354116
Sparse Core Ops, SparseCore 0:
  11.4 56.3 all-gather.4
  82.2 141.4 all-reduce.4
  269.0 53.0 all-gather.6
where the time goes:
time: 357 us
  waiting for transfers between devices  253 us (71%)
  blocking collectives  39.5 us (11%)
  matrix products  23.7 us (7%)
  local copies, waits for them, and re-layouts  18.7 us (5%)
  between operations  13.9 us (4%)
  other arithmetic  8.04 us (2%)
    unnamed x4, waiting for transfers between devices  141 us
    all_gather x1, waiting for transfers between devices, local(): group_normed = lax.all_gather(normed, 'fsdp', axis=0, tiled=True)  58.1 us
    all_gather x1, waiting for transfers between devices, local(): group_grads = lax.all_gather(grad_logits, 'fsdp', axis=0, tiled=True)  53.2 us
    psum x1, blocking collectives, leave_one_out(): divergence = lax.psum(jnp.sum(log_gap[:, None] * inside, axis=0), 'fsdp')  39.5 us
    slice x1, local copies, waits for them, and re-layouts, local(): grad_inner[:, unit_count:]  13.9 us
    dot_general x1, matrix products, local(): lax.dot_general(row_block, gate_grads, (((0,), (0,)), ((), ())), preferre...  7.46 us
  transfers between devices with their start and end apart: 3, of which 3 were waited for; matrix products, arithmetic and copies ran while one was open for 0% of the time, Pallas kernels for 0%

commit v1 on v0

--- a/solution.py
+++ b/solution.py
@@ -70,7 +70,11 @@
 
 
 def leave_one_out(log_gap, inside, prompt_index, rewards):
-    divergence = lax.psum(jnp.sum(log_gap[:, None] * inside, axis=0), "fsdp")
+
+    def close_series_all_on(payload, along_axis):
+        return jnp.sum(lax.all_gather(payload, along_axis), axis=0)
+
+    divergence = close_series_all_on(jnp.sum(log_gap[:, None] * inside, axis=0), "fsdp")
     scores = rewards[0] - KL_WEIGHT * divergence
     same_prompt = (prompt_index[0][:, None] == prompt_index[0][None, :]).astype(jnp.float32)
     others = jnp.sum(same_prompt * scores[None, :], axis=1) - scores

time: 357 us -> 358 us (level)
    psum x1 -> x0, blocking collectives: 39.5 us -> none  [leave_one_out(): divergence = lax.psum(jnp.sum(log_gap[:, None] * inside, axis=0), 'fsdp')]
    unnamed x0 -> x1, blocking collectives: none -> 39.5 us
where the time goes in v1:
time: 358 us; the launch traced here: 357 us
  waiting for transfers between devices  253 us (71%)
  blocking collectives  39.5 us (11%)
  matrix products  23.7 us (7%)
  local copies, waits for them, and re-layouts  19 us (5%)
  between operations  14 us (4%)
  other arithmetic  8.06 us (2%)
    unnamed x4, waiting for transfers between devices  141 us
    all_gather x1, waiting for transfers between devices, local(): group_normed = lax.all_gather(normed, 'fsdp', axis=0, tiled=True)  58.1 us
    all_gather x1, waiting for transfers between devices, local(): group_grads = lax.all_gather(grad_logits, 'fsdp', axis=0, tiled=True)  53.2 us
    unnamed x1, blocking collectives  39.5 us
    slice x1, local copies, waits for them, and re-layouts, local(): grad_inner[:, unit_count:]  13.9 us
    dot_general x1, matrix products, local(): lax.dot_general(row_block, gate_grads, (((0,), (0,)), ((), ())), preferre...  7.46 us
  transfers between devices with their start and end apart: 3, of which 3 were waited for; matrix products, arithmetic and copies ran while one was open for 0% of the time, Pallas kernels for 0%

profile of v1, /device:TPU:0, one launch (start us, length us, event | category | flops | bytes accessed | tf_op | source)
XLA Modules:
  0.0 357.1 jit_solution(13420961613031663541)
XLA Ops:
  7.2 0.9 fusion.12
  8.1 1.5 fusion.15
  9.7 58.1 %all-gather.6.cloned.1.call-done = bf16[32,4,4096]{2,1,0:T(4,128)(2,1)} async-done(((bf16[1,4,4096]{2,1,0:T(4,128)(2,1)}), bf16[32,4,4096]{2,1,0:T(4,128)(2,1)}) %all-gather.6.cloned.1.call-update) | async-done | bytes 1048592 | tf_op jit(solution)/shard_map/all_gather | solution.py:123
  67.8 1.3 reshape.96
  69.1 3.4 fusion.27
  72.5 1.2 multiply_convert_fusion.2
  73.7 0.9 copy-done
  74.6 2.1 fusion.28
  76.7 1.1 copy-done.10
  77.8 2.1 fusion
  80.0 2.1 fusion.9
  82.5 141.3 %all-reduce.6.cloned.1.call-done = (f32[128,4096]{1,0:T(8,128)}, f32[128,4096]{1,0:T(8,128)}) async-done(((f32[128,4096]{1,0:T(8,128)}, f32[128,4096]{1,0:T(8,128)}), (f32[128,4096]{1,0:T(8,128)}, f32[128,4096]{1,0:T(8,128)})) %all-reduce.6.cloned.1.call-update) | async-done | bytes 4194320
  223.8 1.1 fusion.17
  224.9 1.2 exponential_reduce_fusion
  226.1 1.1 exponential_reduce_fusion.1
  227.4 0.2 dynamic-update-slice
  227.6 39.5 %all-reduce = f32[1024]{0:T(1024)S(1)} all-reduce(f32[1024]{0:T(1024)S(1)} %dynamic-update-slice), channel_id=2, replica_groups=mesh['dp'=1,'fsdp'=32] {'fsdp'}, use_global_device_ids=true, to_apply=%add | all-reduce | flops 1024 | bytes 8192
  267.6 1.6 fusion.16
  269.2 53.2 %all-gather.8.cloned.1.call-done = bf16[32,4,4096]{2,1,0:T(4,128)(2,1)} async-done(((bf16[1,4,4096]{2,1,0:T(4,128)(2,1)}), bf16[32,4,4096]{2,1,0:T(4,128)(2,1)}) %all-gather.8.cloned.1.call-update) | async-done | bytes 1048592 | tf_op jit(solution)/shard_map/all_gather | solution.py:156
  322.4 1.3 reshape.98
  323.8 4.3 %fusion.4 = f32[462,4096]{1,0:T(8,128)} fusion(bf16[128,462]{0,1:T(8,128)(2,1)S(1)} %get-tuple-element.20, bf16[128,4096]{1,0:T(8,128)(2,1)S(1)} %reshape.98), kind=kOutput, calls=%fused_computation.6 | convolution fusion | flops 488226816 | bytes 8736256 | tf_op jit(solution)/shard_map/dot_general | solution.py:157
  328.1 1.2 multiply_convert_fusion.1
  329.2 7.5 %convert_convert_fusion = f32[4096,924]{0,1:T(8,128)} fusion(bf16[128,4096]{1,0:T(8,128)(2,1)S(1)} %reshape.96, bf16[128,462]{0,1:T(8,128)(2,1)S(1)} %get-tuple-element.19, bf16[128,462]{0,1:T(8,128)(2,1)S(1)} %get-tuple-element.18), kind=kOutput, calls=%fused_computation.4 | convolution fusion | flops 976926720 | bytes 16423936 | tf_op jit(solution)/shard_map/dot_general | solution.py:174
  336.7 13.9 %fusion.26 = (f32[4096,462]{0,1:T(8,128)}, f32[4096,462]{0,1:T(8,128)}) fusion(f32[4096,924]{0,1:T(8,128)} %convert_convert_fusion), kind=kLoop, calls=%fused_computation.53 | loop fusion | bytes 30277632 | tf_op jit(solution)/shard_map/slice | solution.py:181
  (44 shorter events, 1.0 us)
Async XLA Ops:
  7.2 60.6 %all-gather.6.cloned.1.call-start = ((), (), s32[]{:S(2)}) async-start(), calls=%async_computation | async-start | bytes 1081344 | tf_op jit(solution)/shard_map/all_gather | solution.py:123
  9.6 214.2 %all-reduce.6.cloned.1.call-start = ((), (), s32[]{:S(2)}) async-start(), calls=%async_computation.2 | async-start | bytes 8388608
  69.1 3.4 copy-start.2
  72.5 2.1 copy-start
  72.5 4.1 %copy-start.11 = (bf16[4096,462]{0,1:T(8,128)(2,1)S(1)}, bf16[4096,462]{0,1:T(8,128)(2,1)}, u32[]{:S(2)}) copy-start(bf16[4096,462]{0,1:T(8,128)(2,1)} %param.15) | copy-start | bytes 11354116
  73.7 4.1 %copy-start.10 = (bf16[4096,462]{0,1:T(8,128)(2,1)S(1)}, bf16[4096,462]{0,1:T(8,128)(2,1)}, u32[]{:S(2)}) copy-start(bf16[4096,462]{0,1:T(8,128)(2,1)} %param.16) | copy-start | bytes 11354116
  77.8 2.1 copy-start.3
  79.9 2.2 copy-start.7
  80.0 143.9 %copy-start.4 = (bf16[4,4096]{1,0:T(4,128)(2,1)S(1)}, bf16[4,4096]{1,0:T(4,128)(2,1)}, u32[]{:S(2)}) copy-start(bf16[4,4096]{1,0:T(4,128)(2,1)} %param.12) | copy-start | bytes 98308
  80.0 144.9 %copy-start.5 = (s32[4]{0:T(128)S(1)}, s32[4]{0:T(128)}, u32[]{:S(2)}) copy-start(s32[4]{0:T(128)} %param.13) | copy-start | bytes 52
  82.1 185.1 %copy-start.8 = (f32[1,32]{1,0:T(1,128)S(1)}, f32[1,32]{1,0:T(1,128)}, u32[]{:S(2)}) copy-start(f32[1,32]{1,0:T(1,128)} %param.23) | copy-start | bytes 388
  82.1 185.2 %copy-start.6 = (s32[1,32]{1,0:T(1,128)S(1)}, s32[1,32]{1,0:T(1,128)}, u32[]{:S(2)}) copy-start(s32[1,32]{1,0:T(1,128)} %param.22) | copy-start | bytes 388
  82.1 240.3 %all-gather.8.cloned.1.call-start = ((), (), s32[]{:S(2)}) async-start(), calls=%async_computation.1 | async-start | bytes 1081344 | tf_op jit(solution)/shard_map/all_gather | solution.py:156
  267.4 60.6 %copy-start.9 = (f32[1,32]{1,0:T(1,128)}, f32[1,32]{1,0:T(1,128)S(1)}, u32[]{:S(2)}) copy-start(f32[1,32]{1,0:T(1,128)S(1)} %fusion.20) | copy-start | bytes 388
  323.8 4.3 %copy-start.1 = (bf16[462,4096]{1,0:T(8,128)(2,1)S(1)}, bf16[462,4096]{1,0:T(8,128)(2,1)}, u32[]{:S(2)}) copy-start(bf16[462,4096]{1,0:T(8,128)(2,1)} %param.20) | copy-start | bytes 11354116
Sparse Core Ops, SparseCore 0:
  11.4 56.3 all-gather.5
  82.2 141.5 all-reduce.5
  269.3 53.0 all-gather.7
